TPU v7x, 32 devices: a whole 2x2x4 slice. The times are simulated.
32 devices in a mesh: grp: 2 (over y), ctx: 4 (over z), tp: 2 (over x), sub: 2 (over core).
Axes of the slice: x: 2, y: 2, z: 4, core: 2. Of those that a mesh axis runs over, the one named last changes fastest.
Arguments:
- context: bfloat16 [3072, 2048], P(('grp', 'ctx'), ('tp', 'sub')), parts along dimension 0, may hold values from -24 to 24
- context_pos: int32 [3072], P(('grp', 'ctx')), parts along dimension 0, may hold values from 0 to 1535, each once
- latent_in: bfloat16 [64, 2048], P(('grp', 'ctx')), parts along dimension 0, may hold values from -24 to 24
- latent_start: int32 [2], P('grp'), parts along dimension 0, may hold values from 768 to 1504
- ctx_gain: float32 [2048], replicated, may hold values from 0.25 to 1.75
- lat_gain: float32 [2048], replicated, may hold values from 0.25 to 1.75
- mid_gain: float32 [2048], replicated, may hold values from 0.25 to 1.75
- cross_q: bfloat16 [2048, 2048], P('ctx', ('tp', 'sub')), may hold values from -2 to 2
- cross_k: bfloat16 [2048, 2048], P('ctx', ('tp', 'sub')), may hold values from -2 to 2
- cross_v: bfloat16 [2048, 2048], P('ctx', ('tp', 'sub')), may hold values from -0.125 to 0.125
- cross_out: bfloat16 [2048, 2048], P('ctx', ('tp', 'sub')), may hold values from -0.125 to 0.125
- self_qkv: bfloat16 [2048, 3, 2048], P('ctx', None, ('tp', 'sub')), may hold values from -2 to 2
- self_out: bfloat16 [2048, 2048], P('ctx', ('tp', 'sub')), may hold values from -0.125 to 0.125
Outputs:
- latent_out: bfloat16 [64, 2048], P(('grp', 'ctx'), ('tp', 'sub')), parts along dimension 0
There are 2 independent parts, one for each index of `grp`. A program takes and returns all parts, laid end to end along the dimension named above; an argument that names none is the same for every part. Nothing has to cross between parts.
Inputs may be any that keep to these rules, and one draw needn't show every extreme that they name: context_pos holds each of 0 to 1535 once.
All inputs are finite; a program needn't handle non-finite values.
Results may differ from a plain program's by a relative error of at most 0.035.
Values may be sent and summed in bfloat16 or wider, within the bound.
A program may use at most 64 MiB of HBM per device.

v0:
```python
import math

import jax
import jax.numpy as jnp
from jax import lax
from jax.sharding import PartitionSpec as P

DH = 128


EPS = 1e-05
NEG = -1e30


def combined_all(shard, axis, combine):
    everything = jax.tree.map(
        lambda part, kind: lax.all_gather(part.astype(kind), axis),
        shard,
        (jnp.bfloat16, jnp.bfloat16, jnp.bfloat16),
    )

    def take(k):
        return jax.tree.map(lambda part, own: part[k].astype(own.dtype), everything, shard)

    return lax.fori_loop(
        1, lax.axis_size(axis), lambda k, so_far: combine(so_far, take(k)), take(0)
    )


def rms_rows(values, gain):
    wide = values.astype(jnp.float32)
    scale = lax.rsqrt(jnp.mean(wide * wide, axis=-1, keepdims=True) + EPS)
    return (wide * scale * gain).astype(jnp.bfloat16)


def contract_last(left, right):
    return lax.dot_general(
        left, right, (((1,), (1,)), ((), ())), preferred_element_type=jnp.float32
    )


def softmax_parts(queries, keys, values, allowed):
    heads = queries.shape[1] // DH
    maxima = []
    totals = []
    numerators = []
    for head in range(heads):
        begin = head * DH
        scores = contract_last(queries[:, begin : begin + DH], keys[:, begin : begin + DH]) * (
            1.0 / math.sqrt(DH)
        )
        scores = jnp.where(allowed, scores, NEG)
        top = jnp.max(scores, axis=1)
        weights = jnp.where(allowed, jnp.exp(scores - top[:, None]), 0.0)
        maxima.append(top)
        totals.append(jnp.sum(weights, axis=1))
        numerators.append(
            jnp.dot(
                weights.astype(jnp.bfloat16),
                values[:, begin : begin + DH],
                preferred_element_type=jnp.float32,
            )
        )
    return (
        jnp.stack(maxima, axis=1),
        jnp.stack(totals, axis=1),
        jnp.concatenate(numerators, axis=1),
    )


def combine_parts(first, second):
    top = jnp.maximum(first[0], second[0])
    first_factor = jnp.exp(first[0] - top)
    second_factor = jnp.exp(second[0] - top)
    totals = first[1] * first_factor + second[1] * second_factor
    numerators = first[2] * jnp.repeat(first_factor, DH, axis=1) + second[2] * jnp.repeat(
        second_factor, DH, axis=1
    )
    return (top, totals, numerators)


def on_device(
    context,
    context_pos,
    latent_in,
    latent_start,
    ctx_gain,
    lat_gain,
    mid_gain,
    cross_q,
    cross_k,
    cross_v,
    cross_out,
    self_qkv,
    self_out,
):
    owned = latent_in.shape[0]
    columns = cross_q.shape[1]
    whole = lax.all_gather(context, ("tp", "sub"), axis=1, tiled=True)
    normed_ctx = rms_rows(whole, ctx_gain)
    normed_lat = rms_rows(latent_in, lat_gain)
    query_sum = jnp.dot(
        normed_lat,
        lax.all_gather(cross_q, "ctx", axis=0, tiled=True),
        preferred_element_type=jnp.float32,
    )
    key_sum = jnp.dot(
        normed_ctx,
        lax.all_gather(cross_k, "ctx", axis=0, tiled=True),
        preferred_element_type=jnp.float32,
    )
    value_sum = jnp.dot(
        normed_ctx,
        lax.all_gather(cross_v, "ctx", axis=0, tiled=True),
        preferred_element_type=jnp.float32,
    )
    keys = key_sum.astype(jnp.bfloat16)
    values = value_sum.astype(jnp.bfloat16)
    queries = lax.all_gather(query_sum.astype(jnp.bfloat16), "ctx", axis=0, tiled=True)
    query_pos = latent_start[0] + jnp.arange(queries.shape[0], dtype=jnp.int32)
    allowed = context_pos[None, :] <= query_pos[:, None]
    maxima, totals, numerators = softmax_parts(queries, keys, values, allowed)
    first_row = lax.axis_index("ctx") * owned
    maxima, totals, numerators = combined_all((maxima, totals, numerators), "ctx", combine_parts)
    totals = lax.dynamic_slice_in_dim(totals, first_row, owned, 0)
    numerators = lax.dynamic_slice_in_dim(numerators, first_row, owned, 0)
    attended = (numerators / jnp.repeat(totals, DH, axis=1)).astype(jnp.bfloat16)
    cross_terms = contract_last(attended, lax.all_gather(cross_out, "ctx", axis=0, tiled=True))
    cross_sum = lax.psum(cross_terms.astype(jnp.bfloat16), ("tp", "sub")).astype(jnp.float32)
    hidden = (latent_in.astype(jnp.float32) + cross_sum).astype(jnp.bfloat16)
    normed_mid = rms_rows(hidden, mid_gain)
    piece = lax.all_gather(self_qkv, "ctx", axis=0, tiled=True)
    span = piece.shape[0]
    projected = jnp.dot(
        normed_mid, piece.reshape(span, 3 * columns), preferred_element_type=jnp.float32
    )
    projected = projected.astype(jnp.bfloat16).reshape(owned, 3, columns)
    gathered = lax.all_gather(projected[:, 1:], "ctx", axis=0, tiled=True)
    key_index = jnp.arange(gathered.shape[0], dtype=jnp.int32)
    row_index = first_row + jnp.arange(owned, dtype=jnp.int32)
    causal = key_index[None, :] <= row_index[:, None]
    unused, self_totals, self_numerators = softmax_parts(
        projected[:, 0], gathered[:, 0], gathered[:, 1], causal
    )
    attended_self = (self_numerators / jnp.repeat(self_totals, DH, axis=1)).astype(jnp.bfloat16)
    self_terms = contract_last(attended_self, lax.all_gather(self_out, "ctx", axis=0, tiled=True))
    summed = lax.psum_scatter(
        self_terms.astype(jnp.bfloat16), ("tp", "sub"), scatter_dimension=1, tiled=True
    ).astype(jnp.float32)
    share = summed.shape[1]
    residual = lax.dynamic_slice_in_dim(hidden, lax.axis_index(("tp", "sub")) * share, share, 1)
    return (residual.astype(jnp.float32) + summed).astype(jnp.bfloat16)


def solution(mesh):
    return jax.shard_map(
        on_device,
        mesh=mesh,
        in_specs=(
            P(("grp", "ctx"), ("tp", "sub")),
            P(("grp", "ctx")),
            P(("grp", "ctx"), None),
            P("grp"),
            P(),
            P(),
            P(),
            P("ctx", ("tp", "sub")),
            P("ctx", ("tp", "sub")),
            P("ctx", ("tp", "sub")),
            P("ctx", ("tp", "sub")),
            P("ctx", None, ("tp", "sub")),
            P("ctx", ("tp", "sub")),
        ),
        out_specs=P(("grp", "ctx"), ("tp", "sub")),
        check_vma=False,
    )
```

profile of v0, /device:TPU:0, one launch (start us, length us, event | category | flops | bytes accessed | tf_op | source)
XLA Modules:
  0.0 410.3 jit_solution(3761533873180696968)
XLA Ops:
  6.5 0.7 all-gather.10.cloned.1.call-update
  7.3 0.7 all-gather.8.cloned.1.call-update
  8.1 0.7 all-gather.12.cloned.1.call-update
  8.8 0.5 all-gather.14.cloned.1.call-update
  9.4 0.5 all-gather.16.cloned.1.call-update
  10.0 1.6 copy.21
  11.7 0.7 all-gather.20.cloned.1.call-update
  13.2 18.1 %all-gather.10.cloned.1.call-done = bf16[384,2048]{1,0:T(8,128)(2,1)} async-done(((bf16[384,512]{1,0:T(8,128)(2,1)}), bf16[384,2048]{1,0:T(8,128)(2,1)}) %all-gather.10.cloned.1.call-update) | async-done | bytes 1572880 | tf_op jit(solution)/shard_map/all_gather | solution.py:99
  31.3 1.9 fusion.3
  33.2 45.6 %all-gather.8.cloned.1.call-done = bf16[2048,512]{1,0:T(8,128)(2,1)} async-done(((bf16[512,512]{1,0:T(8,128)(2,1)}), bf16[2048,512]{1,0:T(8,128)(2,1)}) %all-gather.8.cloned.1.call-update) | async-done | bytes 2097168 | tf_op jit(solution)/shard_map/all_gather | solution.py:104
  78.9 2.0 convolution_convert_fusion.9
  80.9 13.3 %all_gather.40 = bf16[32,512]{1,0:T(8,128)(2,1)S(1)} all-gather(bf16[8,512]{1,0:T(8,128)(2,1)S(1)} %convolution_convert_fusion.9), channel_id=1, replica_groups=mesh['grp'=2,'ctx'=4,'tp'=2,'sub'=2] {'ctx'}, dimensions={0}, use_global_device_ids=true | all-gather | bytes 40960 | tf_op jit(solution)/shard_map/all_gather | solution.py:119
  94.2 31.1 %all-gather.12.cloned.1.call-done = bf16[2048,512]{1,0:T(8,128)(2,1)} async-done(((bf16[512,512]{1,0:T(8,128)(2,1)}), bf16[2048,512]{1,0:T(8,128)(2,1)}) %all-gather.12.cloned.1.call-update) | async-done | bytes 2097168 | tf_op jit(solution)/shard_map/all_gather | solution.py:109
  125.3 2.6 convolution_convert_fusion.4
  127.9 0.3 fusion.137
  128.2 0.3 fusion.136
  128.4 0.3 fusion.135
  128.7 0.3 fusion.134
  129.0 42.7 %all-gather.14.cloned.1.call-done = bf16[2048,512]{1,0:T(8,128)(2,1)} async-done(((bf16[512,512]{1,0:T(8,128)(2,1)}), bf16[2048,512]{1,0:T(8,128)(2,1)}) %all-gather.14.cloned.1.call-update) | async-done | bytes 2097168 | tf_op jit(solution)/shard_map/all_gather | solution.py:114
  171.7 2.6 convolution_convert_fusion.3
  174.3 0.2 fusion.10
  174.5 0.2 fusion.11
  174.7 0.2 fusion.12
  174.9 0.2 fusion.13
  175.1 0.2 fusion.36
  175.4 14.4 %all_gather.46 = bf16[4,32,512]{2,1,0:T(8,128)(2,1)S(1)} all-gather(bf16[1,32,512]{2,1,0:T(8,128)(2,1)S(1)} %pad_maximum_fusion), channel_id=1, replica_groups=mesh['grp'=2,'ctx'=4,'tp'=2,'sub'=2] {'ctx'}, dimensions={0}, use_global_device_ids=true | all-gather | bytes 163840 | tf_op jit(solution)/shard_map/all_gather | solution.py:17
  189.9 8.6 %all_gather.44 = bf16[4,32,4]{1,2,0:T(4,128)(2,1)S(1)} all-gather(bf16[1,32,4]{1,2,0:T(4,128)(2,1)S(1)} %pad_maximum_fusion.3), channel_id=1, replica_groups=mesh['grp'=2,'ctx'=4,'tp'=2,'sub'=2] {'ctx'}, dimensions={0}, use_global_device_ids=true | all-gather | bytes 1280 | tf_op jit(solution)/shard_map/all_gather | solution.py:17
  198.5 9.3 %all_gather.43 = bf16[4,32,4]{1,2,0:T(4,128)(2,1)S(1)} all-gather(bf16[1,32,4]{1,2,0:T(4,128)(2,1)S(1)} %pad_maximum_fusion.2), channel_id=1, replica_groups=mesh['grp'=2,'ctx'=4,'tp'=2,'sub'=2] {'ctx'}, dimensions={0}, use_global_device_ids=true | all-gather | bytes 1280 | tf_op jit(solution)/shard_map/all_gather | solution.py:17
  207.8 1.3 while.19
  209.2 9.8 %all-gather.16.cloned.1.call-done = bf16[2048,512]{1,0:T(8,128)(2,1)} async-done(((bf16[512,512]{1,0:T(8,128)(2,1)}), bf16[2048,512]{1,0:T(8,128)(2,1)}) %all-gather.16.cloned.1.call-update) | async-done | bytes 2097168 | tf_op jit(solution)/shard_map/all_gather | solution.py:128
  219.0 2.2 convolution_convert_fusion.2
  221.3 11.4 %psum.7 = bf16[8,2048]{1,0:T(8,128)(2,1)S(1)} all-reduce(bf16[8,2048]{1,0:T(8,128)(2,1)S(1)} %convolution_convert_fusion.2), channel_id=1, replica_groups=mesh['grp'=2,'ctx'=4,'tp'=2,'sub'=2] {'tp','sub'}, use_global_device_ids=true, to_apply=%region_12.13 | all-reduce | flops 16384 | bytes 65536 | tf_op jit(solution)/shard_map/psum | solution.py:129
  232.8 101.9 %all-gather.18.cloned.1.call-done = bf16[2048,3,512]{0,2,1:T(8,128)(2,1)} async-done(((bf16[512,3,512]{0,2,1:T(8,128)(2,1)}), bf16[2048,3,512]{0,2,1:T(8,128)(2,1)}) %all-gather.18.cloned.1.call-update) | async-done | bytes 6291472 | tf_op jit(solution)/shard_map/all_gather | solution.py:132
  334.8 4.5 %convolution_convert_fusion.1 = bf16[8,1536]{1,0:T(8,128)(2,1)S(1)} fusion(bf16[2048,1536]{0,1:T(8,128)(2,1)} %bitcast.107, bf16[8,2048]{1,0:T(8,128)(2,1)S(1)} %get-tuple-element.211, f32[2048]{0:T(1024)S(1)} %copy-done.4, f32[8]{0:T(128)S(1)} %add_rsqrt_fusion.1), kind=kOutput, calls=%fused_computation.16 | convolution fusion | flops 50409472 | bytes 6357024 | tf_op jit(solution)/shard_map/dot_general | solution.py:134
  339.3 13.6 %all_gather.49 = bf16[32,2,512]{2,0,1:T(8,128)(2,1)S(1)} all-gather(bf16[8,2,512]{2,0,1:T(8,128)(2,1)S(1)} %slice.141), channel_id=1, replica_groups=mesh['grp'=2,'ctx'=4,'tp'=2,'sub'=2] {'ctx'}, dimensions={0}, use_global_device_ids=true | all-gather | bytes 81920 | tf_op jit(solution)/shard_map/all_gather | solution.py:138
  352.9 0.2 fusion.141
  353.1 0.2 fusion.140
  353.3 0.2 fusion.139
  353.6 0.2 fusion.138
  353.8 0.2 fusion.92
  354.1 0.2 fusion.83
  354.3 0.2 fusion.80
  354.4 0.2 fusion.77
  354.6 0.2 fusion.74
  354.8 26.4 %all-gather.20.cloned.1.call-done = bf16[2048,512]{1,0:T(8,128)(2,1)} async-done(((bf16[512,512]{1,0:T(8,128)(2,1)}), bf16[2048,512]{1,0:T(8,128)(2,1)}) %all-gather.20.cloned.1.call-update) | async-done | bytes 2097168 | tf_op jit(solution)/shard_map/all_gather | solution.py:146
  381.2 2.9 convolution_convert_fusion
  384.1 18.1 %reduce-scatter.2.cloned.1.call-done = bf16[8,512]{1,0:T(8,128)(2,1)} async-done(((bf16[8,2048]{1,0:T(8,128)(2,1)}), bf16[8,512]{1,0:T(8,128)(2,1)}) %reduce-scatter.2.cloned.1.call-update) | async-done | bytes 8208 | tf_op jit(solution)/shard_map/reduce_scatter | solution.py:147
  402.2 1.3 add_convert_fusion
  (62 shorter events, 2.0 us)
Async XLA Ops:
  6.5 3.4 copy-start
  6.5 24.8 %all-gather.10.cloned.1.call-start = ((), (), s32[]{:S(2)}) async-start(), calls=%async_computation.2 | async-start | bytes 1966080 | tf_op jit(solution)/shard_map/all_gather | solution.py:99
  7.3 71.6 %all-gather.8.cloned.1.call-start = ((), (), s32[]{:S(2)}) async-start(), calls=%async_computation.1 | async-start | bytes 2621440 | tf_op jit(solution)/shard_map/all_gather | solution.py:104
  8.0 117.3 %all-gather.12.cloned.1.call-start = ((), (), s32[]{:S(2)}) async-start(), calls=%async_computation.3 | async-start | bytes 2621440 | tf_op jit(solution)/shard_map/all_gather | solution.py:109
  8.7 162.9 %all-gather.14.cloned.1.call-start = ((), (), s32[]{:S(2)}) async-start(), calls=%async_computation.4 | async-start | bytes 2621440 | tf_op jit(solution)/shard_map/all_gather | solution.py:114
  9.3 209.7 %all-gather.16.cloned.1.call-start = ((), (), s32[]{:S(2)}) async-start(), calls=%async_computation.5 | async-start | bytes 2621440 | tf_op jit(solution)/shard_map/all_gather | solution.py:128
  9.9 3.2 copy-start.2
  9.9 324.8 %all-gather.18.cloned.1.call-start = ((), (), s32[]{:S(2)}) async-start(), calls=%async_computation.6 | async-start | bytes 7864320 | tf_op jit(solution)/shard_map/all_gather | solution.py:132
  11.6 67.3 %copy-start.3 = (f32[2048]{0:T(1024)S(1)}, f32[2048]{0:T(1024)}, u32[]{:S(2)}) copy-start(f32[2048]{0:T(1024)} %param.20) | copy-start | bytes 24580
  11.6 113.7 %copy-start.6 = (f32[2048]{0:T(1024)S(1)}, f32[2048]{0:T(1024)}, u32[]{:S(2)}) copy-start(f32[2048]{0:T(1024)} %param.19) | copy-start | bytes 24580
  11.6 369.6 %all-gather.20.cloned.1.call-start = ((), (), s32[]{:S(2)}) async-start(), calls=%async_computation.7 | async-start | bytes 2621440 | tf_op jit(solution)/shard_map/all_gather | solution.py:146
  12.4 389.8 %reduce-scatter.2.cloned.1.call-start = ((), (), s32[]{:S(2)}) async-start(), calls=%async_computation.8 | async-start | bytes 40960 | tf_op jit(solution)/shard_map/reduce_scatter | solution.py:147
  31.3 94.0 %copy-start.1 = (bf16[384,2048]{1,0:T(8,128)(2,1)S(1)}, bf16[384,2048]{1,0:T(8,128)(2,1)}, u32[]{:S(2)}) copy-start(bf16[384,2048]{1,0:T(8,128)(2,1)} %all-gather.10.cloned.1.call-done) | copy-start | bytes 4718596
  94.2 33.7 %copy-start.5 = (s32[384]{0:T(512)S(1)}, s32[384]{0:T(512)}, u32[]{:S(2)}) copy-start(s32[384]{0:T(512)} %param.16) | copy-start | bytes 4612
  207.8 127.0 %copy-start.4 = (f32[2048]{0:T(1024)S(1)}, f32[2048]{0:T(1024)}, u32[]{:S(2)}) copy-start(f32[2048]{0:T(1024)} %param.21) | copy-start | bytes 24580
Sparse Core Ops, SparseCore 0:
  8.9 22.3 all-gather.9
  32.9 45.9 all-gather.7
  80.4 44.7 all-gather.11
  126.7 44.9 all-gather.13
  173.1 45.9 all-gather.15
  220.5 114.2 all-gather.17
  336.3 44.8 all-gather.19
  384.2 17.9 reduce-scatter.1
where the time goes:
time: 411 us; the launch traced here: 410 us
  waiting for transfers between devices  298 us (73%)
  blocking collectives  70.6 us (17%)
  matrix products  20.4 us (5%)
  between operations  14.3 us (3%)
  other arithmetic  4.19 us (1%)
    all_gather x1, waiting for transfers between devices, on_device(): piece = lax.all_gather(self_qkv, 'ctx', axis=0, tiled=True)  102 us
    all_gather x1, waiting for transfers between devices, on_device(): lax.all_gather(cross_q, 'ctx', axis=0, tiled=True)  45.6 us
    all_gather x1, waiting for transfers between devices, on_device(): lax.all_gather(cross_v, 'ctx', axis=0, tiled=True)  42.7 us
    all_gather x3, blocking collectives, combined_all(): lax.all_gather(part.astype(kind), axis)  32.3 us
    all_gather x1, waiting for transfers between devices, on_device(): lax.all_gather(cross_k, 'ctx', axis=0, tiled=True)  31.1 us
    all_gather x1, waiting for transfers between devices, on_device(): lax.all_gather(self_out, 'ctx', axis=0, tiled=True)  26.4 us
    reduce_scatter x1, waiting for transfers between devices, on_device(): lax.psum_scatter(self_terms.astype(jnp.bfloat16), ('tp', 'sub'), scatter_...  18.1 us
    all_gather x1, waiting for transfers between devices, on_device(): whole = lax.all_gather(context, ('tp', 'sub'), axis=1, tiled=True)  18.1 us
  transfers between devices with their start and end apart: 8, of which 8 were waited for; matrix products, arithmetic and copies ran while one was open for 6% of the time, Pallas kernels for 0%

commit v1 on v0

v1 whole, which is shorter than its diff:
```python
import math

import jax
import jax.numpy as jnp
from jax import lax
from jax.sharding import PartitionSpec as P

DH = 128


EPS = 1e-05
NEG = -1e30
HEADS_AXES = ("tp", "sub")


def contract_last(left, right):
    return lax.dot_general(
        left, right, (((1,), (1,)), ((), ())), preferred_element_type=jnp.float32
    )


def summed_over(partial, axis):
    everything = lax.all_gather(partial.astype(jnp.bfloat16), axis)
    return jnp.sum(everything.astype(jnp.float32), axis=0)


def on_device(
    context,
    context_pos,
    latent_in,
    latent_start,
    ctx_gain,
    lat_gain,
    mid_gain,
    cross_q,
    cross_k,
    cross_v,
    cross_out,
    self_qkv,
    self_out,
):
    rows, width = latent_in.shape
    depth, columns = cross_q.shape
    shards = lax.axis_size("ctx")
    heads = columns // DH
    latents = rows * shards
    own = lax.axis_index("ctx")
    mine = lambda array: lax.dynamic_slice_in_dim(array, own * depth, depth, array.ndim - 1)
    whole = lax.all_gather(context, HEADS_AXES, axis=1, tiled=True)
    all_latents = lax.all_gather(latent_in, "ctx", axis=0, tiled=True).astype(jnp.float32)
    lat_scale = lax.rsqrt(jnp.mean(all_latents * all_latents, axis=1, keepdims=True) + EPS)
    lat_part = mine(all_latents)
    normed_lat = (lat_part * lat_scale * mine(lat_gain)).astype(jnp.bfloat16)
    queries = summed_over(
        jnp.dot(normed_lat, cross_q, preferred_element_type=jnp.float32), "ctx"
    ).astype(jnp.bfloat16)
    split = [slice(head * DH, head * DH + DH) for head in range(heads)]
    absorbed = jnp.concatenate(
        [contract_last(queries[:, cut], cross_k[:, cut]) for cut in split], axis=0
    )
    absorbed = (absorbed * (mine(ctx_gain) * (1.0 / math.sqrt(DH)))).astype(jnp.bfloat16)
    absorbed = lax.all_gather(absorbed, "ctx", axis=1, tiled=True)

    wide = whole.astype(jnp.float32)
    token_scale = lax.rsqrt(jnp.mean(wide * wide, axis=1) + EPS)
    scores = contract_last(absorbed, whole) * token_scale[None, :]
    query_pos = latent_start[0] + jnp.arange(latents, dtype=jnp.int32)
    allowed = jnp.tile(context_pos[None, :] <= query_pos[:, None], (heads, 1))
    scores = jnp.where(allowed, scores, NEG)
    top = jnp.max(scores, axis=1, keepdims=True)
    weights = jnp.where(allowed, jnp.exp(scores - top), 0.0)
    total = jnp.sum(weights, axis=1, keepdims=True)
    mixed = jnp.dot(
        (weights * token_scale[None, :]).astype(jnp.bfloat16),
        whole,
        preferred_element_type=jnp.float32,
    ).astype(jnp.bfloat16)
    mixed = lax.all_to_all(
        mixed.reshape(heads * latents, shards, depth), "ctx", split_axis=1, concat_axis=0
    ).reshape(shards, heads * latents, depth)
    stats = lax.all_gather(jnp.concatenate([top, total], axis=1), "ctx")
    tops, totals = stats[:, :, :1], stats[:, :, 1:]
    factors = jnp.exp(tops - jnp.max(tops, axis=0))
    mixed = jnp.sum(mixed.astype(jnp.float32) * factors, axis=0) / jnp.sum(totals * factors, axis=0)
    mixed = (mixed * mine(ctx_gain)).astype(jnp.bfloat16)
    attended = jnp.concatenate(
        [
            jnp.dot(
                mixed[head * latents : (head + 1) * latents],
                cross_v[:, cut],
                preferred_element_type=jnp.float32,
            )
            for head, cut in enumerate(split)
        ],
        axis=1,
    )
    attended = summed_over(attended, "ctx").astype(jnp.bfloat16)
    cross_sum = summed_over(contract_last(attended, cross_out), HEADS_AXES)
    hidden = (lat_part + cross_sum).astype(jnp.bfloat16).astype(jnp.float32)
    squares = jnp.sum(lax.all_gather(jnp.sum(hidden * hidden, axis=1), "ctx"), axis=0)
    hidden_scale = lax.rsqrt(squares / width + EPS)
    projected = jnp.dot(
        (hidden * mine(mid_gain)).astype(jnp.bfloat16),
        self_qkv.reshape(depth, 3 * columns),
        preferred_element_type=jnp.float32,
    )
    projected = summed_over(projected, "ctx") * hidden_scale[:, None]
    projected = projected.astype(jnp.bfloat16).reshape(latents, 3, columns)
    index = jnp.arange(latents, dtype=jnp.int32)
    causal = index[None, :] <= index[:, None]
    parts = []
    for cut in split:
        scores = contract_last(projected[:, 0, cut], projected[:, 1, cut]) * (1.0 / math.sqrt(DH))
        scores = jnp.where(causal, scores, NEG)
        weights = jnp.where(causal, jnp.exp(scores - jnp.max(scores, axis=1, keepdims=True)), 0.0)
        numerator = jnp.dot(
            weights.astype(jnp.bfloat16), projected[:, 2, cut], preferred_element_type=jnp.float32
        )
        parts.append(numerator / jnp.sum(weights, axis=1, keepdims=True))
    attended_self = jnp.concatenate(parts, axis=1).astype(jnp.bfloat16)
    self_sum = summed_over(contract_last(attended_self, self_out), HEADS_AXES)
    result = (hidden + self_sum).astype(jnp.bfloat16)
    result = lax.all_to_all(
        result.reshape(shards, rows, depth), "ctx", split_axis=0, concat_axis=1
    ).reshape(rows, width)
    return lax.dynamic_slice_in_dim(result, lax.axis_index(HEADS_AXES) * columns, columns, 1)


def solution(mesh):
    return jax.shard_map(
        on_device,
        mesh=mesh,
        in_specs=(
            P(("grp", "ctx"), ("tp", "sub")),
            P(("grp", "ctx")),
            P(("grp", "ctx"), None),
            P("grp"),
            P(),
            P(),
            P(),
            P("ctx", ("tp", "sub")),
            P("ctx", ("tp", "sub")),
            P("ctx", ("tp", "sub")),
            P("ctx", ("tp", "sub")),
            P("ctx", None, ("tp", "sub")),
            P("ctx", ("tp", "sub")),
        ),
        out_specs=P(("grp", "ctx"), ("tp", "sub")),
        check_vma=False,
    )
```

time: 411 us -> 153 us (0.37)
  waiting for transfers between devices: 298 us -> 6.38 us
  blocking collectives: 70.6 us -> 104 us
  matrix products: 20.4 us -> 8.52 us
  starting transfers between devices: 0.27 us -> 8.01 us
    all_gather x7 -> x1, waiting for transfers between devices: 276 us -> 0.01 us  [on_device(): whole = lax.all_gather(context, HEADS_AXES, axis=1, tiled=True)]
    all_gather x5 -> x8, blocking collectives: 59.2 us -> 95.5 us  [the longest x5 53.4 us: summed_over(): everything = lax.all_gather(partial.astype(jnp.bfloat16), axis)]
    reduce_scatter x1 -> x0, waiting for transfers between devices: 18.1 us -> none  [on_device(): lax.psum_scatter(self_terms.astype(jnp.bfloat16), ('tp', 'sub'), scatter_...]
    psum x1 -> x0, blocking collectives: 11.4 us -> none  [on_device(): lax.psum(cross_terms.astype(jnp.bfloat16), ('tp', 'sub'))]
    unnamed x0 -> x1, blocking collectives: none -> 8.34 us
    all_to_all x0 -> x2, starting transfers between devices: none -> 8.01 us  [the longest x1 4.73 us: on_device(): lax.all_to_all(mixed.reshape(heads * latents, shards, depth), 'ctx', spli...]
    dot_general x12 -> x11, matrix products: 13.3 us -> 6.11 us  [the longest x4 4.18 us: on_device(): jnp.dot(mixed[head * latents:(head + 1) * latents], cross_v[:, cut], pref...]
    all_to_all x0 -> x2, waiting for transfers between devices: none -> 5.66 us  [the longest x1 5.66 us: on_device(): lax.all_to_all(result.reshape(shards, rows, depth), 'ctx', split_axis=0,...]
  transfers between devices with their start and end apart: 8 -> 3, of which waited for: 8 -> 1; matrix products, arithmetic and copies ran while one was open for 6% -> 4% of each run, Pallas kernels for 0% -> 0%
where the time goes in v1:
time: 153 us
  blocking collectives  104 us (68%)
  between operations  14.9 us (10%)
  matrix products  8.52 us (6%)
  starting transfers between devices  8.01 us (5%)
  local copies, waits for them, and re-layouts  6.4 us (4%)
  waiting for transfers between devices  6.38 us (4%)
  other arithmetic  4.64 us (3%)
    all_gather x5, blocking collectives, summed_over(): everything = lax.all_gather(partial.astype(jnp.bfloat16), axis)  53.4 us
    all_gather x1, blocking collectives, on_device(): absorbed = lax.all_gather(absorbed, 'ctx', axis=1, tiled=True)  15.5 us
    all_gather x1, blocking collectives, on_device(): lax.all_gather(latent_in, 'ctx', axis=0, tiled=True).astype(jnp.float32)  15.3 us
    all_gather x1, blocking collectives, on_device(): stats = lax.all_gather(jnp.concatenate([top, total], axis=1), 'ctx')  11.4 us
    unnamed x1, blocking collectives  8.34 us
    all_to_all x1, waiting for transfers between devices, on_device(): lax.all_to_all(result.reshape(shards, rows, depth), 'ctx', split_axis=0,...  5.66 us
    all_to_all x1, starting transfers between devices, on_device(): lax.all_to_all(mixed.reshape(heads * latents, shards, depth), 'ctx', spli...  4.73 us
    dot_general x4, matrix products, on_device(): jnp.dot(mixed[head * latents:(head + 1) * latents], cross_v[:, cut], pref...  4.18 us
  transfers between devices with their start and end apart: 3, of which 1 were waited for; matrix products, arithmetic and copies ran while one was open for 4% of the time, Pallas kernels for 0%

profile of v1, /device:TPU:0, one launch (start us, length us, event | category | flops | bytes accessed | tf_op | source)
XLA Modules:
  0.0 152.7 jit_solution(14311558146944119064)
XLA Ops:
  6.5 0.7 all-gather.8.cloned.1.call-update
  7.3 15.3 %all_gather.49 = bf16[32,2048]{1,0:T(8,128)(2,1)S(1)} all-gather(bf16[8,2048]{1,0:T(8,128)(2,1)} %param.15), channel_id=1, replica_groups=mesh['grp'=2,'ctx'=4,'tp'=2,'sub'=2] {'ctx'}, dimensions={0}, use_global_device_ids=true | all-gather | bytes 163840 | tf_op jit(solution)/shard_map/all_gather | solution.py:50
  23.4 0.8 dynamic_slice.17
  24.1 0.2 convolution_convert_fusion.4
  24.4 13.7 %all-gather = bf16[128,512]{1,0:T(8,128)(2,1)S(1)} all-gather(bf16[32,512]{1,0:T(8,128)(2,1)S(1)} %convolution_convert_fusion.4), channel_id=2, replica_groups=mesh['grp'=2,'ctx'=4,'tp'=2,'sub'=2] {'ctx'}, dimensions={0}, use_global_device_ids=true | all-gather | bytes 163840 | tf_op jit(solution)/shard_map/all_gather | solution.py:23
  38.1 0.8 broadcast_multiply_fusion
  39.0 0.2 fusion.22
  39.2 0.2 fusion.24
  39.3 0.2 fusion.26
  39.5 15.5 %all_gather.52 = bf16[128,2048]{1,0:T(8,128)(2,1)S(1)} all-gather(bf16[128,512]{1,0:T(8,128)(2,1)S(1)} %fusion.14), channel_id=1, replica_groups=mesh['grp'=2,'ctx'=4,'tp'=2,'sub'=2] {'ctx'}, dimensions={1}, use_global_device_ids=true | all-gather | bytes 655360 | tf_op jit(solution)/shard_map/all_gather | solution.py:62
  55.1 1.9 %multiply_reduce_fusion = f32[384]{0:T(512)S(1)} fusion(bf16[384,2048]{1,0:T(8,128)(2,1)} %all-gather.8.cloned.1.call-done), kind=kLoop, calls=%fused_computation | loop fusion | flops 2358912 | bytes 1574400 | tf_op jit(solution)/shard_map/reduce_sum | solution.py:65
  57.1 0.7 fusion.104
  57.8 0.2 fusion.15
  58.0 0.5 convolution_convert_fusion
  58.4 0.4 broadcast_in_dim_reshape.6
  58.8 0.9 copy.17
  59.7 4.7 %all-to-all-start = ((bf16[1,128,4,512]{3,1,0,2:T(8,128)(2,1)}), bf16[1,128,4,512]{3,1,0,2:T(8,128)(2,1)S(1)}, u32[]{:S(2)}, u32[]{:S(2)}) async-start(bf16[1,128,4,512]{3,1,0,2:T(8,128)(2,1)} %copy.17), calls=%async_computation | async-start | bytes 1048576 | tf_op jit(solution)/shard_map/all_to_all | solution.py:78
  64.4 0.8 dynamic_slice.19
  65.2 1.7 %copy.18 = bf16[512,3,512]{0,2,1:T(8,128)(2,1)S(1)} copy(bf16[512,3,512]{2,0,1:T(8,128)(2,1)} %param.24) | data formatting | bytes 3145728 | tf_op args[11]
  67.0 0.6 dynamic-slice
  68.2 11.4 %all-gather.1 = f32[512,2]{0,1:T(2,128)S(1)} all-gather(f32[128,2]{0,1:T(2,128)S(1)} %pad_maximum_fusion.1), channel_id=3, replica_groups=mesh['grp'=2,'ctx'=4,'tp'=2,'sub'=2] {'ctx'}, dimensions={0}, use_global_device_ids=true | all-gather | bytes 5120 | tf_op jit(solution)/shard_map/all_gather | solution.py:81
  79.7 0.2 fusion.13
  80.0 1.0 fusion.10
  81.0 1.0 fusion.11
  82.0 1.0 fusion.12
  83.1 1.0 fusion.9
  84.2 13.4 %all_gather.56 = bf16[4,32,512]{2,1,0:T(8,128)(2,1)S(1)} all-gather(bf16[1,32,512]{2,1,0:T(8,128)(2,1)S(1)} %pad_maximum_fusion), channel_id=1, replica_groups=mesh['grp'=2,'ctx'=4,'tp'=2,'sub'=2] {'ctx'}, dimensions={0}, use_global_device_ids=true | all-gather | bytes 163840 | tf_op jit(solution)/shard_map/all_gather | solution.py:23
  97.6 0.2 convolution_convert_fusion.3
  97.8 5.4 %all-gather.2 = bf16[128,512]{1,0:T(8,128)(2,1)S(1)} all-gather(bf16[32,512]{1,0:T(8,128)(2,1)S(1)} %convolution_convert_fusion.3), channel_id=4, replica_groups=mesh['grp'=2,'ctx'=4,'tp'=2,'sub'=2] {'tp','sub'}, dimensions={0}, use_global_device_ids=true | all-gather | bytes 163840 | tf_op jit(solution)/shard_map/all_gather | solution.py:23
  103.4 0.6 convolution_convert_fusion.1
  104.0 15.4 %all-gather.3 = bf16[128,1536]{1,0:T(8,128)(2,1)S(1)} all-gather(bf16[32,1536]{1,0:T(8,128)(2,1)S(1)} %convolution_convert_fusion.1), channel_id=5, replica_groups=mesh['grp'=2,'ctx'=4,'tp'=2,'sub'=2] {'ctx'}, dimensions={0}, use_global_device_ids=true | all-gather | bytes 491520 | tf_op jit(solution)/shard_map/all_gather | solution.py:23
  119.4 0.1 reduce_sum.161
  119.6 0.2 dynamic-update-slice
  119.8 8.3 %all-reduce = f32[128]{0:T(128)S(1)} all-reduce(f32[128]{0:T(128)S(1)} %dynamic-update-slice), channel_id=6, replica_groups=mesh['grp'=2,'ctx'=4,'tp'=2,'sub'=2] {'ctx'}, use_global_device_ids=true, to_apply=%add | all-reduce | flops 128 | bytes 1024
  128.4 0.2 fusion.103
  128.7 0.2 fusion.5
  128.9 0.2 fusion.107
  129.1 0.2 fusion.6
  129.3 0.2 fusion.106
  129.5 0.2 fusion.7
  129.7 0.2 fusion.105
  129.8 0.2 fusion.8
  130.0 0.3 convolution_convert_fusion.2
  130.3 5.4 %all-gather.5 = bf16[128,512]{1,0:T(8,128)(2,1)S(1)} all-gather(bf16[32,512]{1,0:T(8,128)(2,1)S(1)} %convolution_convert_fusion.2), channel_id=7, replica_groups=mesh['grp'=2,'ctx'=4,'tp'=2,'sub'=2] {'tp','sub'}, dimensions={0}, use_global_device_ids=true | all-gather | bytes 163840 | tf_op jit(solution)/shard_map/all_gather | solution.py:23
  135.7 0.6 fusion.31
  136.4 3.3 %all-to-all-start.1 = ((bf16[4,8,1,512]{3,1,2,0:T(8,128)(2,1)}), bf16[4,8,1,512]{3,1,2,0:T(8,128)(2,1)S(1)}, u32[]{:S(2)}, u32[]{:S(2)}) async-start(bf16[4,8,1,512]{3,1,2,0:T(8,128)(2,1)} %fusion.31), calls=%async_computation.1 | async-start | bytes 65536 | tf_op jit(solution)/shard_map/all_to_all | solution.py:123
  139.6 5.7 %all-to-all-done.1 = bf16[4,8,1,512]{3,1,2,0:T(8,128)(2,1)S(1)} async-done(((bf16[4,8,1,512]{3,1,2,0:T(8,128)(2,1)}), bf16[4,8,1,512]{3,1,2,0:T(8,128)(2,1)S(1)}, u32[]{:S(2)}, u32[]{:S(2)}) %all-to-all-start.1) | async-done | bytes 32800 | tf_op jit(solution)/shard_map/all_to_all | solution.py:123
  145.3 0.6 constant_dynamic-slice_fusion
  (48 shorter events, 1.4 us)
Async XLA Ops:
  6.5 17.6 %copy-start = (bf16[512,512]{1,0:T(8,128)(2,1)S(1)}, bf16[512,512]{1,0:T(8,128)(2,1)}, u32[]{:S(2)}) copy-start(bf16[512,512]{1,0:T(8,128)(2,1)} %param.20) | copy-start | bytes 1572868
  6.5 32.3 %copy-start.4 = (bf16[512,512]{1,0:T(8,128)(2,1)S(1)}, bf16[512,512]{1,0:T(8,128)(2,1)}, u32[]{:S(2)}) copy-start(bf16[512,512]{1,0:T(8,128)(2,1)} %param.21) | copy-start | bytes 1572868
  6.5 48.6 %all-gather.8.cloned.1.call-start = ((), (), s32[]{:S(2)}) async-start(), calls=%async_computation.2 | async-start | bytes 1966080 | tf_op jit(solution)/shard_map/all_gather | solution.py:49
  22.7 32.4 %copy-start.5 = (s32[384]{0:T(512)S(1)}, s32[384]{0:T(512)}, u32[]{:S(2)}) copy-start(s32[384]{0:T(512)} %param.14) | copy-start | bytes 4612
  55.1 2.0 %copy-start.1 = (bf16[384,2048]{1,0:T(8,128)(2,1)S(1)}, bf16[384,2048]{1,0:T(8,128)(2,1)}, u32[]{:S(2)}) copy-start(bf16[384,2048]{1,0:T(8,128)(2,1)} %all-gather.8.cloned.1.call-done) | copy-start | bytes 4718596
  59.7 20.0 %all-to-all-start = ((bf16[1,128,4,512]{3,1,0,2:T(8,128)(2,1)}), bf16[1,128,4,512]{3,1,0,2:T(8,128)(2,1)S(1)}, u32[]{:S(2)}, u32[]{:S(2)}) async-start(bf16[1,128,4,512]{3,1,0,2:T(8,128)(2,1)} %copy.17), calls=%async_computation | async-start | bytes 1048576 | tf_op jit(solution)/shard_map/all_to_all | solution.py:78
  65.2 1.8 %copy-start.6 = (u32[32]{0:T(128)S(1)}, u32[32]{0:T(128)}, u32[]{:S(2)}) copy-start(u32[32]{0:T(128)} %constant.45) | copy-start | bytes 388
  66.9 30.7 %copy-start.2 = (bf16[512,512]{1,0:T(8,128)(2,1)S(1)}, bf16[512,512]{1,0:T(8,128)(2,1)}, u32[]{:S(2)}) copy-start(bf16[512,512]{1,0:T(8,128)(2,1)} %param.23) | copy-start | bytes 1572868
  104.0 26.0 %copy-start.3 = (bf16[512,512]{1,0:T(8,128)(2,1)S(1)}, bf16[512,512]{1,0:T(8,128)(2,1)}, u32[]{:S(2)}) copy-start(bf16[512,512]{1,0:T(8,128)(2,1)} %param.25) | copy-start | bytes 1572868
  136.4 8.9 %all-to-all-start.1 = ((bf16[4,8,1,512]{3,1,2,0:T(8,128)(2,1)}), bf16[4,8,1,512]{3,1,2,0:T(8,128)(2,1)S(1)}, u32[]{:S(2)}, u32[]{:S(2)}) async-start(bf16[4,8,1,512]{3,1,2,0:T(8,128)(2,1)} %fusion.31), calls=%async_computation.1 | async-start | bytes 65536 | tf_op jit(solution)/shard_map/all_to_all | solution.py:123
Sparse Core Ops, SparseCore 0:
  8.9 22.3 all-gather.7

commit v2 on v1

--- a/solution.py
+++ b/solution.py
@@ -3,6 +3,8 @@
 import jax
 import jax.numpy as jnp
 from jax import lax
+from jax.experimental import pallas as pl
+from jax.experimental.pallas import tpu as pltpu
 from jax.sharding import PartitionSpec as P
 
 DH = 128
@@ -11,6 +13,7 @@
 EPS = 1e-05
 NEG = -1e30
 HEADS_AXES = ("tp", "sub")
+MESH = pl.DeviceIdType.MESH
 
 
 def contract_last(left, right):
@@ -24,7 +27,7 @@
     return jnp.sum(everything.astype(jnp.float32), axis=0)
 
 
-def on_device(
+def collectives(
     context,
     context_pos,
     latent_in,
@@ -126,6 +129,471 @@
     return lax.dynamic_slice_in_dim(result, lax.axis_index(HEADS_AXES) * columns, columns, 1)
 
 
+def step_kernel(
+    start_ref,
+    pos_ref,
+    latent_ref,
+    gain_ref,
+    context_ref,
+    q_hbm,
+    k_hbm,
+    v_hbm,
+    out_hbm,
+    qkv_hbm,
+    last_hbm,
+    result_ref,
+    ctx_buf,
+    q_ref,
+    k_ref,
+    v_ref,
+    o_ref,
+    qkv_ref,
+    last_ref,
+    lat_stage,
+    lat_buf,
+    query_stage,
+    query_buf,
+    absorbed_buf,
+    stat_stage,
+    stat_buf,
+    mixed_stage,
+    mixed_buf,
+    att_stage,
+    att_buf,
+    cross_stage,
+    cross_buf,
+    proj_stage,
+    proj_buf,
+    square_stage,
+    square_buf,
+    end_stage,
+    end_buf,
+    load_sem,
+    ring_send,
+    ring_recv,
+    ctx_send,
+    ctx_recv,
+    cross_send,
+    cross_recv,
+    end_send,
+    end_recv,
+):
+    shards, tps, subs = lax.axis_size("ctx"), lax.axis_size("tp"), lax.axis_size("sub")
+    peers = tps * subs
+    own, tp, sub = lax.axis_index("ctx"), lax.axis_index("tp"), lax.axis_index("sub")
+    spot = tp * subs + sub
+    rows, width = latent_ref.shape
+    depth, columns = q_ref.shape
+    heads = columns // DH
+    latents = rows * shards
+    tokens = context_ref.shape[0]
+    ratio = columns // depth
+    f32, bf16 = jnp.float32, jnp.bfloat16
+    split = [slice(head * DH, head * DH + DH) for head in range(heads)]
+
+    loads = [
+        pltpu.make_async_copy(source, target, load_sem.at[index])
+        for index, (source, target) in enumerate(
+            (
+                (context_ref, ctx_buf.at[spot]),
+                (q_hbm, q_ref),
+                (k_hbm, k_ref),
+                (v_hbm, v_ref),
+                (out_hbm, o_ref),
+                (qkv_hbm, qkv_ref),
+                (last_hbm, last_ref),
+            )
+        )
+    ]
+    for load in loads:
+        load.start()
+
+    barrier = pltpu.get_barrier_semaphore()
+    everyone = shards * peers
+    me = own * peers + spot
+    for step in range(1, everyone):
+        other = lax.rem(me + step, everyone)
+        pl.semaphore_signal(
+            barrier,
+            inc=1,
+            device_id={
+                "ctx": other // peers,
+                "tp": lax.rem(other, peers) // subs,
+                "sub": lax.rem(other, subs),
+            },
+            device_id_type=MESH,
+        )
+
+    wide = latent_ref[...].astype(f32)
+    scale = lax.rsqrt(jnp.mean(wide * wide, axis=1, keepdims=True) + EPS)
+    for shard in range(shards):
+        part = wide[:, shard * depth : (shard + 1) * depth]
+        lat_stage[shard] = jnp.concatenate(
+            [part, part * scale * gain_ref[1, shard]], axis=0
+        ).astype(bf16)
+    pl.semaphore_wait(barrier, everyone - 1)
+
+    started = []
+
+    def send(source, target, send_sem, recv_sem, device):
+        copy = pltpu.make_async_remote_copy(
+            src_ref=source,
+            dst_ref=target,
+            send_sem=send_sem,
+            recv_sem=recv_sem,
+            device_id=device,
+            device_id_type=MESH,
+        )
+        copy.start()
+        started.append(copy)
+        return copy
+
+    def ring(phase, pick, target):
+        return [
+            send(
+                pick(lax.rem(own + step, shards)),
+                target(step),
+                ring_send.at[phase, step],
+                ring_recv.at[phase, step],
+                {"ctx": lax.rem(own + step, shards)},
+            )
+            for step in range(1, shards)
+        ]
+
+    def arrive(copies):
+        for copy in copies:
+            copy.wait_recv()
+
+    def summed(first, buf):
+        for step in range(1, buf.shape[0]):
+            first = first + buf[step].astype(f32)
+        return first
+
+    moved = ring(0, lambda peer: lat_stage.at[peer], lambda step: lat_buf.at[own])
+    across = [
+        send(
+            context_ref,
+            ctx_buf.at[spot],
+            ctx_send.at[0, step],
+            ctx_recv.at[0, step],
+            {"tp": lax.rem(tp + step, tps)},
+        )
+        for step in range(1, tps)
+    ]
+    beside = [
+        send(
+            context_ref,
+            ctx_buf.at[spot],
+            ctx_send.at[tps, step],
+            ctx_recv.at[tps, step],
+            {"sub": lax.rem(sub + step, subs)},
+        )
+        for step in range(1, subs)
+    ]
+    lat_buf[own] = lat_stage[own]
+    loads[1].wait()
+    arrive(moved)
+    blocks = [lat_buf[shard].astype(f32) for shard in range(shards)]
+    lat_part = jnp.concatenate([block[:rows] for block in blocks], axis=0)
+    normed = jnp.concatenate([block[rows:] for block in blocks], axis=0).astype(bf16)
+    partial = jnp.dot(normed, q_ref[...], preferred_element_type=f32)
+    query_stage[...] = partial.astype(bf16)
+    moved = ring(1, lambda peer: query_stage, lambda step: query_buf.at[step])
+    loads[2].wait()
+    arrive(moved)
+    queries = summed(partial, query_buf).astype(bf16)
+    absorbed = jnp.concatenate(
+        [contract_last(queries[:, cut], k_ref[:, cut]) for cut in split], axis=0
+    )
+    absorbed_buf[own] = (absorbed * (gain_ref[0, own] * (1.0 / math.sqrt(DH)))).astype(bf16)
+    moved = ring(2, lambda peer: absorbed_buf.at[own], lambda step: absorbed_buf.at[own])
+
+    for step, copy in enumerate(across, 1):
+        copy.wait_recv()
+        block = lax.rem(tp + tps - step, tps) * subs + sub
+        beside = beside + [
+            send(
+                ctx_buf.at[block],
+                ctx_buf.at[block],
+                ctx_send.at[step, hop],
+                ctx_recv.at[step, hop],
+                {"sub": lax.rem(sub + hop, subs)},
+            )
+            for hop in range(1, subs)
+        ]
+    loads[0].wait()
+    arrive(beside)
+    squares = jnp.zeros((8, tokens), f32)
+    for block in range(peers):
+        wide = ctx_buf[block].astype(f32)
+        squares = squares + lax.dot_general(
+            jnp.ones((8, columns), f32),
+            wide * wide,
+            (((1,), (1,)), ((), ())),
+            precision=lax.Precision.HIGHEST,
+            preferred_element_type=f32,
+        )
+    token_scale = lax.rsqrt(squares[:1] / width + EPS)
+    query_pos = start_ref[0] + lax.broadcasted_iota(jnp.int32, (latents, tokens), 0)
+    query_pos = jnp.concatenate([query_pos] * heads, axis=0)
+    allowed = jnp.broadcast_to(pos_ref[...], query_pos.shape) <= query_pos
+    arrive(moved)
+
+    def features(shard):
+        inside = shard % ratio * depth
+        return ctx_buf[shard // ratio][:, inside : inside + depth]
+
+    scores = contract_last(absorbed_buf[0], features(0))
+    for shard in range(1, shards):
+        scores = scores + contract_last(absorbed_buf[shard], features(shard))
+    scores = jnp.where(allowed, scores * token_scale, NEG)
+    top = jnp.max(scores, axis=1, keepdims=True)
+    weights = jnp.where(allowed, jnp.exp(scores - top), 0.0)
+    total = jnp.sum(weights, axis=1, keepdims=True)
+    lane = lax.broadcasted_iota(jnp.int32, (heads * latents, 128), 1)
+    stat_stage[...] = jnp.transpose(jnp.where(lane == 0, top, total))[:8]
+    moved = ring(3, lambda peer: stat_stage, lambda step: stat_buf.at[step])
+    scaled = (weights * token_scale).astype(bf16)
+    for shard in range(shards):
+        mixed_stage[shard] = jnp.dot(
+            scaled, features(shard), preferred_element_type=f32
+        ).astype(bf16)
+    moved = moved + ring(4, lambda peer: mixed_stage.at[peer], lambda step: mixed_buf.at[step])
+    stat_buf[0] = stat_stage[...]
+    mixed_buf[0] = mixed_stage[own]
+    loads[3].wait()
+    arrive(moved)
+    tops = jnp.concatenate([stat_buf[step][0:1] for step in range(shards)], axis=0)
+    totals = jnp.concatenate([stat_buf[step][1:2] for step in range(shards)], axis=0)
+    factors = jnp.exp(tops - jnp.max(tops, axis=0, keepdims=True))
+    factors = factors / jnp.sum(totals * factors, axis=0, keepdims=True)
+    short = -shards % 128
+    factors = jnp.transpose(
+        jnp.concatenate([factors, jnp.zeros((short, factors.shape[1]), f32)], axis=0)
+    )
+    mixed = mixed_buf[0].astype(f32) * factors[:, 0:1]
+    for step in range(1, shards):
+        mixed = mixed + mixed_buf[step].astype(f32) * factors[:, step : step + 1]
+    mixed = (mixed * gain_ref[0, own]).astype(bf16)
+    partial = jnp.concatenate(
+        [
+            jnp.dot(
+                mixed[head * latents : (head + 1) * latents],
+                v_ref[:, cut],
+                preferred_element_type=f32,
+            )
+            for head, cut in enumerate(split)
+        ],
+        axis=1,
+    )
+    att_stage[...] = partial.astype(bf16)
+    moved = ring(5, lambda peer: att_stage, lambda step: att_buf.at[step])
+    loads[4].wait()
+    arrive(moved)
+    attended = summed(partial, att_buf).astype(bf16)
+    partial = contract_last(attended, o_ref[...])
+    cross_stage[...] = partial.astype(bf16)
+    moved = []
+    for step in range(1, peers):
+        other = lax.rem(spot + step, peers)
+        moved.append(
+            send(
+                cross_stage,
+                cross_buf.at[step],
+                cross_send.at[step],
+                cross_recv.at[step],
+                {"tp": other // subs, "sub": lax.rem(other, subs)},
+            )
+        )
+    loads[5].wait()
+    arrive(moved)
+    hidden = (lat_part + summed(partial, cross_buf)).astype(bf16).astype(f32)
+    scaled = (hidden * gain_ref[2, own]).astype(bf16)
+    partials = [
+        jnp.dot(scaled, qkv_ref[index], preferred_element_type=f32) for index in range(3)
+    ]
+    partial = jnp.concatenate(partials, axis=1)
+    proj_stage[...] = partial.astype(bf16)
+    square = jnp.broadcast_to(
+        jnp.sum(hidden * hidden, axis=1, keepdims=True), square_stage.shape
+    )
+    square_stage[...] = square
+    moved = ring(6, lambda peer: square_stage, lambda step: square_buf.at[step])
+    moved = moved + ring(7, lambda peer: proj_stage, lambda step: proj_buf.at[step])
+    loads[6].wait()
+    arrive(moved)
+    hidden_scale = lax.rsqrt(summed(square, square_buf)[:, :1] / width + EPS)
+    projected = (summed(partial, proj_buf) * hidden_scale).astype(bf16)
+    causal = lax.broadcasted_iota(jnp.int32, (latents, latents), 1) <= lax.broadcasted_iota(
+        jnp.int32, (latents, latents), 0
+    )
+    parts = []
+    for head in range(heads):
+        self_q, self_k, self_v = (
+            projected[:, at * columns + head * DH : at * columns + (head + 1) * DH]
+            for at in range(3)
+        )
+        scores = contract_last(self_q, self_k) * (1.0 / math.sqrt(DH))
+        scores = jnp.where(causal, scores, NEG)
+        weights = jnp.where(causal, jnp.exp(scores - jnp.max(scores, axis=1, keepdims=True)), 0.0)
+        numerator = jnp.dot(weights.astype(bf16), self_v, preferred_element_type=f32)
+        parts.append(numerator / jnp.sum(weights, axis=1, keepdims=True))
+    attended = jnp.concatenate(parts, axis=1).astype(bf16)
+    partial = contract_last(attended, last_ref[...])
+    partial = partial + hidden * jnp.where(spot == 0, 1.0, 0.0).astype(f32)
+
+    goal = own // ratio
+    slot = lax.rem(own, ratio) * peers + spot
+    for shard in range(shards):
+        end_stage[shard] = partial[shard * rows : (shard + 1) * rows]
+
+    def hand(step):
+        other = lax.rem(own + step, shards)
+        return pltpu.make_async_remote_copy(
+            src_ref=end_stage.at[other],
+            dst_ref=end_buf.at[slot],
+            send_sem=end_send.at[step],
+            recv_sem=end_recv.at[slot],
+            device_id={"ctx": other, "tp": goal // subs, "sub": lax.rem(goal, subs)},
+            device_id_type=MESH,
+        )
+
+    for step in range(1, shards):
+        hand(step).start()
+
+    @pl.when(goal != spot)
+    def _():
+        hand(0).start()
+
+    @pl.when(goal == spot)
+    def _():
+        end_buf[slot] = end_stage[own]
+
+    for inside in range(ratio):
+        for source in range(peers):
+            at = inside * peers + source
+
+            @pl.when(jnp.logical_or(spot * ratio + inside != own, spot != source))
+            def _():
+                pltpu.make_async_remote_copy(
+                    src_ref=end_stage.at[0],
+                    dst_ref=end_buf.at[at],
+                    send_sem=end_send.at[0],
+                    recv_sem=end_recv.at[at],
+                    device_id={"ctx": lax.rem(own + 1, shards)},
+                    device_id_type=MESH,
+                ).wait_recv()
+
+    for inside in range(ratio):
+        first = end_buf[inside * peers]
+        for source in range(1, peers):
+            first = first + end_buf[inside * peers + source]
+        result_ref[:, inside * depth : (inside + 1) * depth] = first.astype(bf16)
+    for copy in started:
+        copy.wait_send()
+    for step in range(1, shards):
+        hand(step).wait_send()
+
+    @pl.when(goal != spot)
+    def _():
+        hand(0).wait_send()
+
+
+def fused(
+    context,
+    context_pos,
+    latent_in,
+    latent_start,
+    ctx_gain,
+    lat_gain,
+    mid_gain,
+    cross_q,
+    cross_k,
+    cross_v,
+    cross_out,
+    self_qkv,
+    self_out,
+):
+    rows, width = latent_in.shape
+    depth, columns = cross_q.shape
+    tokens = context.shape[0]
+    shards, tps, subs = lax.axis_size("ctx"), lax.axis_size("tp"), lax.axis_size("sub")
+    peers = tps * subs
+    latents = rows * shards
+    lines = columns // DH * latents
+    ends = columns // depth * peers
+    gains = jnp.stack([ctx_gain, lat_gain, mid_gain]).reshape(3, shards, 1, depth)
+    f32, bf16 = jnp.float32, jnp.bfloat16
+    vmem, dma = pltpu.VMEM, pltpu.SemaphoreType.DMA
+    held = pl.BlockSpec(memory_space=pltpu.VMEM)
+    away = pl.BlockSpec(memory_space=pl.ANY)
+    return pl.pallas_call(
+        step_kernel,
+        out_shape=jax.ShapeDtypeStruct((rows, columns), bf16),
+        in_specs=[pl.BlockSpec(memory_space=pltpu.SMEM)] + [held] * 3 + [away] * 7,
+        out_specs=held,
+        scratch_shapes=[
+            vmem((peers, tokens, columns), bf16),
+            vmem((depth, columns), bf16),
+            vmem((depth, columns), bf16),
+            vmem((depth, columns), bf16),
+            vmem((depth, columns), bf16),
+            vmem((3, depth, columns), bf16),
+            vmem((depth, columns), bf16),
+            vmem((shards, 2 * rows, depth), bf16),
+            vmem((shards, 2 * rows, depth), bf16),
+            vmem((latents, columns), bf16),
+            vmem((shards, latents, columns), bf16),
+            vmem((shards, lines, depth), bf16),
+            vmem((8, lines), f32),
+            vmem((shards, 8, lines), f32),
+            vmem((shards, lines, depth), bf16),
+            vmem((shards, lines, depth), bf16),
+            vmem((latents, columns), bf16),
+            vmem((shards, latents, columns), bf16),
+            vmem((latents, depth), bf16),
+            vmem((peers, latents, depth), bf16),
+            vmem((latents, 3 * columns), bf16),
+            vmem((shards, latents, 3 * columns), bf16),
+            vmem((latents, 128), f32),
+            vmem((shards, latents, 128), f32),
+            vmem((shards, rows, depth), f32),
+            vmem((ends, rows, depth), f32),
+            dma((7,)),
+            dma((8, shards)),
+            dma((8, shards)),
+            dma((tps + 1, max(tps, subs))),
+            dma((tps + 1, max(tps, subs))),
+            dma((peers,)),
+            dma((peers,)),
+            dma((shards,)),
+            dma((ends,)),
+        ],
+        compiler_params=pltpu.CompilerParams(
+            collective_id=0, has_side_effects=True, vmem_limit_bytes=56 << 20
+        ),
+    )(
+        latent_start,
+        context_pos.reshape(1, tokens),
+        latent_in,
+        gains,
+        context,
+        cross_q,
+        cross_k,
+        cross_v,
+        cross_out,
+        jnp.transpose(self_qkv, (1, 0, 2)),
+        self_out,
+    )
+
+
+def on_device(*arrays):
+    depth, columns = arrays[7].shape
+    if depth % 128 == 0 and columns % depth == 0:
+        return fused(*arrays)
+    return collectives(*arrays)
+
+
 def solution(mesh):
     return jax.shard_map(
         on_device,

time: 153 us -> 74.1 us (0.48)
  the two profiles are of different devices: /device:TPU:0 before, /device:TPU:7 now
where the time goes in v2:
time: 74.1 us; the launch traced here: 73.8 us
  Pallas kernels  69.2 us (93%)
  local copies, waits for them, and re-layouts  2.54 us (3%)
  other arithmetic  1.35 us (2%)
    pallas_call x1, Pallas kernels, fused(): pl.pallas_call(step_kernel, out_shape=jax.ShapeDtypeStruct((rows, columns...  69.2 us

profile of v2, /device:TPU:7, one launch (start us, length us, event | category | flops | bytes accessed | tf_op | source)
XLA Modules:
  0.0 73.8 jit_solution(11952744668474571761)
XLA Ops:
  0.7 1.2 %reshape.10.pos_ref = s32[1,384]{1,0:T(1,128)} reshape(s32[384]{0:T(512)} %param.14) | data formatting | bytes 3072 | tf_op jit(solution)/shard_map/reshape | solution.py:577
  1.9 1.3 %pad_maximum_fusion.gain_ref = f32[3,4,1,512]{3,2,1,0:T(1,128)} fusion(f32[1,4,1,512]{3,2,1,0:T(1,128)} %bitcast.5, f32[1,4,1,512]{3,2,1,0:T(1,128)} %bitcast.6, f32[1,4,1,512]{3,2,1,0:T(1,128)} %bitcast.7), kind=kLoop, calls=%fused_computation | loop fusion | flops 12288 | bytes 49152 | tf_op jit(solution)/shard_map/stack | solution.py:525
  3.2 69.2 %shard_map.127 = bf16[8,512]{1,0:T(8,128)(2,1)} custom-call(s32[1]{0:T(128)S(6)} %copy.15.start_ref, s32[1,384]{1,0:T(1,128)} %reshape.10.pos_ref, bf16[8,2048]{1,0:T(8,128)(2,1)} %latent_ref.1, f32[3,4,1,512]{3,2,1,0:T(1,128)} %pad_maximum_fusion.gain_ref, bf16[384,512]{1,0:T(8,128)(2,1)} %context_ref.1, bf16[512,512]{1,0:T(8,128)(2,1)} %q_hbm.1, ...), custom_call_target="tpu_custom_call" | custom-call | tf_op jit(solution)/shard_map/pallas_call | solution.py:530
  72.5 1.3 %copy.16 = bf16[8,512]{1,0:T(8,128)(2,1)} copy(bf16[8,512]{1,0:T(8,128)(2,1)} %shard_map.127) | data formatting | bytes 16384

commit v3 on v2

--- a/solution.py
+++ b/solution.py
@@ -14,6 +14,7 @@
 NEG = -1e30
 HEADS_AXES = ("tp", "sub")
 MESH = pl.DeviceIdType.MESH
+CHUNKS = 4
 
 
 def contract_last(left, right):
@@ -133,7 +134,9 @@
     start_ref,
     pos_ref,
     latent_ref,
-    gain_ref,
+    ctx_gain_ref,
+    lat_gain_ref,
+    mid_gain_ref,
     context_ref,
     q_hbm,
     k_hbm,
@@ -164,8 +167,7 @@
     cross_buf,
     proj_stage,
     proj_buf,
-    square_stage,
-    square_buf,
+    self_buf,
     end_stage,
     end_buf,
     load_sem,
@@ -229,7 +231,7 @@
     for shard in range(shards):
         part = wide[:, shard * depth : (shard + 1) * depth]
         lat_stage[shard] = jnp.concatenate(
-            [part, part * scale * gain_ref[1, shard]], axis=0
+            [part, part * scale * lat_gain_ref[shard]], axis=0
         ).astype(bf16)
     pl.semaphore_wait(barrier, everyone - 1)
 
@@ -270,26 +272,49 @@
         return first
 
     moved = ring(0, lambda peer: lat_stage.at[peer], lambda step: lat_buf.at[own])
+    chunk = tokens // CHUNKS
+    pieces = [pl.ds(piece * chunk, chunk) for piece in range(CHUNKS)]
     across = [
-        send(
-            context_ref,
-            ctx_buf.at[spot],
-            ctx_send.at[0, step],
-            ctx_recv.at[0, step],
-            {"tp": lax.rem(tp + step, tps)},
-        )
-        for step in range(1, tps)
+        [
+            send(
+                context_ref.at[piece],
+                ctx_buf.at[spot, piece],
+                ctx_send.at[0, step, at],
+                ctx_recv.at[0, step, at],
+                {"tp": lax.rem(tp + step, tps)},
+            )
+            for step in range(1, tps)
+        ]
+        for at, piece in enumerate(pieces)
     ]
     beside = [
         send(
             context_ref,
             ctx_buf.at[spot],
-            ctx_send.at[tps, step],
-            ctx_recv.at[tps, step],
+            ctx_send.at[tps, step, 0],
+            ctx_recv.at[tps, step, 0],
             {"sub": lax.rem(sub + step, subs)},
         )
         for step in range(1, subs)
     ]
+
+    def forward(at):
+        handed = []
+        for step, copy in enumerate(across[at], 1):
+            copy.wait_recv()
+            block = lax.rem(tp + tps - step, tps) * subs + sub
+            handed = handed + [
+                send(
+                    ctx_buf.at[block, pieces[at]],
+                    ctx_buf.at[block, pieces[at]],
+                    ctx_send.at[step, hop, at],
+                    ctx_recv.at[step, hop, at],
+                    {"sub": lax.rem(sub + hop, subs)},
+                )
+                for hop in range(1, subs)
+            ]
+        return handed
+
     lat_buf[own] = lat_stage[own]
     loads[1].wait()
     arrive(moved)
@@ -299,28 +324,19 @@
     partial = jnp.dot(normed, q_ref[...], preferred_element_type=f32)
     query_stage[...] = partial.astype(bf16)
     moved = ring(1, lambda peer: query_stage, lambda step: query_buf.at[step])
+    beside = beside + forward(0)
     loads[2].wait()
     arrive(moved)
+    beside = beside + forward(1)
     queries = summed(partial, query_buf).astype(bf16)
     absorbed = jnp.concatenate(
         [contract_last(queries[:, cut], k_ref[:, cut]) for cut in split], axis=0
     )
-    absorbed_buf[own] = (absorbed * (gain_ref[0, own] * (1.0 / math.sqrt(DH)))).astype(bf16)
+    absorbed_buf[own] = (absorbed * (ctx_gain_ref[own] * (1.0 / math.sqrt(DH)))).astype(bf16)
     moved = ring(2, lambda peer: absorbed_buf.at[own], lambda step: absorbed_buf.at[own])
 
-    for step, copy in enumerate(across, 1):
-        copy.wait_recv()
-        block = lax.rem(tp + tps - step, tps) * subs + sub
-        beside = beside + [
-            send(
-                ctx_buf.at[block],
-                ctx_buf.at[block],
-                ctx_send.at[step, hop],
-                ctx_recv.at[step, hop],
-                {"sub": lax.rem(sub + hop, subs)},
-            )
-            for hop in range(1, subs)
-        ]
+    for at in range(2, CHUNKS):
+        beside = beside + forward(at)
     loads[0].wait()
     arrive(beside)
     squares = jnp.zeros((8, tokens), f32)
@@ -336,16 +352,12 @@
     token_scale = lax.rsqrt(squares[:1] / width + EPS)
     query_pos = start_ref[0] + lax.broadcasted_iota(jnp.int32, (latents, tokens), 0)
     query_pos = jnp.concatenate([query_pos] * heads, axis=0)
-    allowed = jnp.broadcast_to(pos_ref[...], query_pos.shape) <= query_pos
-    arrive(moved)
-
-    def features(shard):
-        inside = shard % ratio * depth
-        return ctx_buf[shard // ratio][:, inside : inside + depth]
-
-    scores = contract_last(absorbed_buf[0], features(0))
-    for shard in range(1, shards):
-        scores = scores + contract_last(absorbed_buf[shard], features(shard))
+    allowed = jnp.broadcast_to(pos_ref[...].reshape(1, tokens), query_pos.shape) <= query_pos
+    scores = contract_last(absorbed_buf[own], ctx_buf[own])
+    for step, copy in enumerate(moved, 1):
+        copy.wait_recv()
+        source = lax.rem(own + shards - step, shards)
+        scores = scores + contract_last(absorbed_buf[source], ctx_buf[source])
     scores = jnp.where(allowed, scores * token_scale, NEG)
     top = jnp.max(scores, axis=1, keepdims=True)
     weights = jnp.where(allowed, jnp.exp(scores - top), 0.0)
@@ -354,13 +366,23 @@
     stat_stage[...] = jnp.transpose(jnp.where(lane == 0, top, total))[:8]
     moved = ring(3, lambda peer: stat_stage, lambda step: stat_buf.at[step])
     scaled = (weights * token_scale).astype(bf16)
-    for shard in range(shards):
-        mixed_stage[shard] = jnp.dot(
-            scaled, features(shard), preferred_element_type=f32
+    mixing = []
+    for step in range(1, shards):
+        other = lax.rem(own + step, shards)
+        mixed_stage[step] = jnp.dot(
+            scaled, ctx_buf[other], preferred_element_type=f32
         ).astype(bf16)
-    moved = moved + ring(4, lambda peer: mixed_stage.at[peer], lambda step: mixed_buf.at[step])
+        mixing.append(
+            send(
+                mixed_stage.at[step],
+                mixed_buf.at[step],
+                ring_send.at[4, step],
+                ring_recv.at[4, step],
+                {"ctx": other},
+            )
+        )
+    mixed = jnp.dot(scaled, ctx_buf[own], preferred_element_type=f32)
     stat_buf[0] = stat_stage[...]
-    mixed_buf[0] = mixed_stage[own]
     loads[3].wait()
     arrive(moved)
     tops = jnp.concatenate([stat_buf[step][0:1] for step in range(shards)], axis=0)
@@ -371,10 +393,11 @@
     factors = jnp.transpose(
         jnp.concatenate([factors, jnp.zeros((short, factors.shape[1]), f32)], axis=0)
     )
-    mixed = mixed_buf[0].astype(f32) * factors[:, 0:1]
-    for step in range(1, shards):
+    mixed = mixed * factors[:, 0:1]
+    for step, copy in enumerate(mixing, 1):
+        copy.wait_recv()
         mixed = mixed + mixed_buf[step].astype(f32) * factors[:, step : step + 1]
-    mixed = (mixed * gain_ref[0, own]).astype(bf16)
+    mixed = (mixed * ctx_gain_ref[own]).astype(bf16)
     partial = jnp.concatenate(
         [
             jnp.dot(
@@ -408,37 +431,37 @@
     loads[5].wait()
     arrive(moved)
     hidden = (lat_part + summed(partial, cross_buf)).astype(bf16).astype(f32)
-    scaled = (hidden * gain_ref[2, own]).astype(bf16)
+    scaled = (hidden * mid_gain_ref[own]).astype(bf16)
     partials = [
         jnp.dot(scaled, qkv_ref[index], preferred_element_type=f32) for index in range(3)
     ]
-    partial = jnp.concatenate(partials, axis=1)
-    proj_stage[...] = partial.astype(bf16)
-    square = jnp.broadcast_to(
-        jnp.sum(hidden * hidden, axis=1, keepdims=True), square_stage.shape
-    )
-    square_stage[...] = square
-    moved = ring(6, lambda peer: square_stage, lambda step: square_buf.at[step])
-    moved = moved + ring(7, lambda peer: proj_stage, lambda step: proj_buf.at[step])
+    square = jnp.sum(hidden * hidden, axis=1, keepdims=True)
+    coarse = square.astype(bf16).astype(f32)
+    lane = lax.broadcasted_iota(jnp.int32, (latents, 128), 1)
+    square = jnp.where(lane == 0, coarse, jnp.where(lane == 1, square - coarse, 0.0))
+    for head, cut in enumerate(split):
+        proj_stage[head] = jnp.concatenate(
+            [part[:, cut] for part in partials] + [square], axis=1
+        ).astype(bf16)
+    moved = ring(6, lambda peer: proj_stage.at[peer], lambda step: proj_buf.at[step])
+    total = proj_stage[own].astype(f32)
     loads[6].wait()
     arrive(moved)
-    hidden_scale = lax.rsqrt(summed(square, square_buf)[:, :1] / width + EPS)
-    projected = (summed(partial, proj_buf) * hidden_scale).astype(bf16)
+    total = summed(total, proj_buf)
+    square = total[:, 3 * DH : 3 * DH + 1] + total[:, 3 * DH + 1 : 3 * DH + 2]
+    projected = (total[:, : 3 * DH] * lax.rsqrt(square / width + EPS)).astype(bf16)
     causal = lax.broadcasted_iota(jnp.int32, (latents, latents), 1) <= lax.broadcasted_iota(
         jnp.int32, (latents, latents), 0
     )
-    parts = []
-    for head in range(heads):
-        self_q, self_k, self_v = (
-            projected[:, at * columns + head * DH : at * columns + (head + 1) * DH]
-            for at in range(3)
-        )
-        scores = contract_last(self_q, self_k) * (1.0 / math.sqrt(DH))
-        scores = jnp.where(causal, scores, NEG)
-        weights = jnp.where(causal, jnp.exp(scores - jnp.max(scores, axis=1, keepdims=True)), 0.0)
-        numerator = jnp.dot(weights.astype(bf16), self_v, preferred_element_type=f32)
-        parts.append(numerator / jnp.sum(weights, axis=1, keepdims=True))
-    attended = jnp.concatenate(parts, axis=1).astype(bf16)
+    scores = contract_last(projected[:, :DH], projected[:, DH : 2 * DH]) * (1.0 / math.sqrt(DH))
+    scores = jnp.where(causal, scores, NEG)
+    weights = jnp.where(causal, jnp.exp(scores - jnp.max(scores, axis=1, keepdims=True)), 0.0)
+    numerator = jnp.dot(
+        weights.astype(bf16), projected[:, 2 * DH :], preferred_element_type=f32
+    )
+    self_buf[own] = (numerator / jnp.sum(weights, axis=1, keepdims=True)).astype(bf16)
+    arrive(ring(7, lambda peer: self_buf.at[own], lambda step: self_buf.at[own]))
+    attended = jnp.concatenate([self_buf[head] for head in range(heads)], axis=1)
     partial = contract_last(attended, last_ref[...])
     partial = partial + hidden * jnp.where(spot == 0, 1.0, 0.0).astype(f32)
 
@@ -522,7 +545,6 @@
     latents = rows * shards
     lines = columns // DH * latents
     ends = columns // depth * peers
-    gains = jnp.stack([ctx_gain, lat_gain, mid_gain]).reshape(3, shards, 1, depth)
     f32, bf16 = jnp.float32, jnp.bfloat16
     vmem, dma = pltpu.VMEM, pltpu.SemaphoreType.DMA
     held = pl.BlockSpec(memory_space=pltpu.VMEM)
@@ -530,7 +552,7 @@
     return pl.pallas_call(
         step_kernel,
         out_shape=jax.ShapeDtypeStruct((rows, columns), bf16),
-        in_specs=[pl.BlockSpec(memory_space=pltpu.SMEM)] + [held] * 3 + [away] * 7,
+        in_specs=[pl.BlockSpec(memory_space=pltpu.SMEM)] + [held] * 5 + [away] * 7,
         out_specs=held,
         scratch_shapes=[
             vmem((peers, tokens, columns), bf16),
@@ -553,17 +575,16 @@
             vmem((shards, latents, columns), bf16),
             vmem((latents, depth), bf16),
             vmem((peers, latents, depth), bf16),
-            vmem((latents, 3 * columns), bf16),
-            vmem((shards, latents, 3 * columns), bf16),
-            vmem((latents, 128), f32),
-            vmem((shards, latents, 128), f32),
+            vmem((shards, latents, 4 * DH), bf16),
+            vmem((shards, latents, 4 * DH), bf16),
+            vmem((shards, latents, DH), bf16),
             vmem((shards, rows, depth), f32),
             vmem((ends, rows, depth), f32),
             dma((7,)),
             dma((8, shards)),
             dma((8, shards)),
-            dma((tps + 1, max(tps, subs))),
-            dma((tps + 1, max(tps, subs))),
+            dma((tps + 1, max(tps, subs), CHUNKS)),
+            dma((tps + 1, max(tps, subs), CHUNKS)),
             dma((peers,)),
             dma((peers,)),
             dma((shards,)),
@@ -574,9 +595,11 @@
         ),
     )(
         latent_start,
-        context_pos.reshape(1, tokens),
+        context_pos,
         latent_in,
-        gains,
+        ctx_gain.reshape(shards, 1, depth),
+        lat_gain.reshape(shards, 1, depth),
+        mid_gain.reshape(shards, 1, depth),
         context,
         cross_q,
         cross_k,
@@ -589,7 +612,7 @@
 
 def on_device(*arrays):
     depth, columns = arrays[7].shape
-    if depth % 128 == 0 and columns % depth == 0:
+    if depth == columns == lax.axis_size("ctx") * DH:
         return fused(*arrays)
     return collectives(*arrays)
 

time: 74.1 us -> 67.2 us (0.907)
  the two profiles are of different devices: /device:TPU:7 before, /device:TPU:0 now
where the time goes in v3:
time: 67.2 us; the launch traced here: 66.9 us
  Pallas kernels  65 us (97%)
  local copies, waits for them, and re-layouts  1.3 us (2%)
    pallas_call x1, Pallas kernels, fused(): pl.pallas_call(step_kernel, out_shape=jax.ShapeDtypeStruct((rows, columns...  65 us

profile of v3, /device:TPU:0, one launch (start us, length us, event | category | flops | bytes accessed | tf_op | source)
XLA Modules:
  0.0 66.9 jit_solution(1778735887652581520)
XLA Ops:
  0.7 65.0 %shard_map.127 = bf16[8,512]{1,0:T(8,128)(2,1)} custom-call(s32[1]{0:T(128)S(6)} %copy.15.start_ref, s32[384]{0:T(512)} %pos_ref.1, bf16[8,2048]{1,0:T(8,128)(2,1)} %latent_ref.1, f32[4,1,512]{2,1,0:T(1,128)} %bitcast.5, f32[4,1,512]{2,1,0:T(1,128)} %bitcast.6, f32[4,1,512]{2,1,0:T(1,128)} %bitcast.7, bf16[384,512]{1,0:T(8,128)(2,1)} %context_ref.1, ...), custom_call_target="tpu_custom_call" | custom-call | tf_op jit(solution)/shard_map/pallas_call | solution.py:552
  65.6 1.3 %copy.16 = bf16[8,512]{1,0:T(8,128)(2,1)} copy(bf16[8,512]{1,0:T(8,128)(2,1)} %shard_map.127) | data formatting | bytes 16384

commit v4 on v3

--- a/solution.py
+++ b/solution.py
@@ -350,7 +350,7 @@
             preferred_element_type=f32,
         )
     token_scale = lax.rsqrt(squares[:1] / width + EPS)
-    query_pos = start_ref[0] + lax.broadcasted_iota(jnp.int32, (latents, tokens), 0)
+    query_pos = start_ref[...].reshape(1, 1) + lax.broadcasted_iota(jnp.int32, (latents, tokens), 0)
     query_pos = jnp.concatenate([query_pos] * heads, axis=0)
     allowed = jnp.broadcast_to(pos_ref[...].reshape(1, tokens), query_pos.shape) <= query_pos
     scores = contract_last(absorbed_buf[own], ctx_buf[own])
@@ -468,7 +468,7 @@
     goal = own // ratio
     slot = lax.rem(own, ratio) * peers + spot
     for shard in range(shards):
-        end_stage[shard] = partial[shard * rows : (shard + 1) * rows]
+        end_stage[shard] = partial[shard * rows : (shard + 1) * rows].astype(bf16)
 
     def hand(step):
         other = lax.rem(own + step, shards)
@@ -508,9 +508,9 @@
                 ).wait_recv()
 
     for inside in range(ratio):
-        first = end_buf[inside * peers]
+        first = end_buf[inside * peers].astype(f32)
         for source in range(1, peers):
-            first = first + end_buf[inside * peers + source]
+            first = first + end_buf[inside * peers + source].astype(f32)
         result_ref[:, inside * depth : (inside + 1) * depth] = first.astype(bf16)
     for copy in started:
         copy.wait_send()
@@ -552,7 +552,7 @@
     return pl.pallas_call(
         step_kernel,
         out_shape=jax.ShapeDtypeStruct((rows, columns), bf16),
-        in_specs=[pl.BlockSpec(memory_space=pltpu.SMEM)] + [held] * 5 + [away] * 7,
+        in_specs=[held] * 6 + [away] * 7,
         out_specs=held,
         scratch_shapes=[
             vmem((peers, tokens, columns), bf16),
@@ -578,8 +578,8 @@
             vmem((shards, latents, 4 * DH), bf16),
             vmem((shards, latents, 4 * DH), bf16),
             vmem((shards, latents, DH), bf16),
-            vmem((shards, rows, depth), f32),
-            vmem((ends, rows, depth), f32),
+            vmem((shards, rows, depth), bf16),
+            vmem((ends, rows, depth), bf16),
             dma((7,)),
             dma((8, shards)),
             dma((8, shards)),

time: 67.2 us -> 67.1 us (level)
  no operation moved by 1% of the time
where the time goes in v4:
time: 67.1 us; the launch traced here: 66.8 us
  Pallas kernels  64.9 us (97%)
  local copies, waits for them, and re-layouts  1.3 us (2%)
    pallas_call x1, Pallas kernels, fused(): pl.pallas_call(step_kernel, out_shape=jax.ShapeDtypeStruct((rows, columns...  64.9 us

profile of v4, /device:TPU:0, one launch (start us, length us, event | category | flops | bytes accessed | tf_op | source)
XLA Modules:
  0.0 66.8 jit_solution(7565833525358523168)
XLA Ops:
  0.7 64.9 %shard_map.127 = bf16[8,512]{1,0:T(8,128)(2,1)} custom-call(s32[1]{0:T(128)S(6)} %copy.15.start_ref, s32[384]{0:T(512)} %pos_ref.1, bf16[8,2048]{1,0:T(8,128)(2,1)} %latent_ref.1, f32[4,1,512]{2,1,0:T(1,128)} %bitcast.5, f32[4,1,512]{2,1,0:T(1,128)} %bitcast.6, f32[4,1,512]{2,1,0:T(1,128)} %bitcast.7, bf16[384,512]{1,0:T(8,128)(2,1)} %context_ref.1, ...), custom_call_target="tpu_custom_call" | custom-call | tf_op jit(solution)/shard_map/pallas_call | solution.py:552
  65.5 1.3 %copy.16 = bf16[8,512]{1,0:T(8,128)(2,1)} copy(bf16[8,512]{1,0:T(8,128)(2,1)} %shard_map.127) | data formatting | bytes 16384
